TPU v7x, 512 devices: a whole 4x4x16 slice. The times are simulated.
512 devices in a mesh: seq: 64 (over x, z), chan: 8 (over y, core).
Axes of the slice: x: 4, y: 4, z: 16, core: 2. Of those that a mesh axis runs over, the one named last changes fastest.
Arguments:
- key_gate: bfloat16 [16384, 8192], P('seq', 'chan'), may hold values from -6 to 6
- values: bfloat16 [16384, 8192], P('seq', 'chan'), may hold values from -6 to 6
- query_gate: bfloat16 [16384, 8192], P('seq', 'chan'), may hold values from -6 to 6
- grad_output: bfloat16 [16384, 8192], P(('seq', 'chan')), may hold values from -6 to 6
- short_taps: bfloat16 [7, 8192], P(None, 'chan'), may hold values from -2 to 2
- long_taps: bfloat16 [128, 8192], P(None, 'chan'), may hold values from -0.5 to 0.5
Outputs:
- grad_query: bfloat16 [16384, 8192], P('seq', 'chan')
- grad_key: bfloat16 [16384, 8192], P('seq', 'chan')
- grad_value: bfloat16 [16384, 8192], P('seq', 'chan')
- grad_long: float32 [128, 8192], P('seq', 'chan')
- grad_short: float32 [7, 8192], P(None, 'chan')
All inputs are finite; a program needn't handle non-finite values.
Results may differ from a plain program's by a relative error of at most 0.0059.
Values may be sent and summed in bfloat16 or wider, within the bound.
A program may use at most 64 MiB of HBM per device.

v0:
```python
import jax
import jax.numpy as jnp
from jax import lax
from jax.sharding import PartitionSpec as P


def passed_along(shard, axis, by):
    length = lax.axis_size(axis)
    pairs = [(i, i + by) for i in range(length) if 0 <= i + by < length]
    return lax.ppermute(shard, axis, pairs)


def depthwise(extended, kernel):
    channels = kernel.shape[2]
    result = lax.conv_general_dilated(
        extended[None],
        kernel,
        (1,),
        [(0, 0)],
        dimension_numbers=("NWC", "WIO", "NWC"),
        feature_group_count=channels,
        preferred_element_type=jnp.float32,
    )
    return result[0]


def causal_apply(extended, weights):
    return depthwise(extended, jnp.flip(weights, 0)[:, None, :])


def forward_apply(extended, weights):
    return depthwise(extended, weights[:, None, :])


def filter_partial(history, grad):
    return jnp.flip(depthwise(history, grad[:, None, :]), 0)


def body(key_gate, values, query_gate, grad_output, short_taps, long_taps):
    long_len = long_taps.shape[0]
    short_len = short_taps.shape[0]
    row_count = key_gate.shape[0]
    cotangent = lax.all_to_all(grad_output, "chan", split_axis=1, concat_axis=0, tiled=True)
    product = (key_gate.astype(jnp.float32) * values.astype(jnp.float32)).astype(jnp.bfloat16)
    grad_mixed = (cotangent.astype(jnp.float32) * query_gate.astype(jnp.float32)).astype(
        jnp.bfloat16
    )
    short_hist = passed_along(product[row_count - (short_len - 1) :], "seq", 1)
    short_ext = jnp.concatenate([short_hist, product], 0)
    short_out = causal_apply(short_ext, short_taps).astype(jnp.bfloat16)
    long_hist = passed_along(short_out[row_count - (long_len - 1) :], "seq", 1)
    long_ext = jnp.concatenate([long_hist, short_out], 0)
    head_long = passed_along(grad_mixed[: long_len - 1], "seq", -1)
    long_back = jnp.concatenate([grad_mixed, head_long], 0)
    grad_conv = forward_apply(long_back, long_taps).astype(jnp.bfloat16)
    head_short = passed_along(grad_conv[: short_len - 1], "seq", -1)
    short_back = jnp.concatenate([grad_conv, head_short], 0)
    mixed = causal_apply(long_ext, long_taps)
    grad_query = (cotangent.astype(jnp.float32) * mixed).astype(jnp.bfloat16)
    grad_product = forward_apply(short_back, short_taps)
    grad_key = (grad_product * values.astype(jnp.float32)).astype(jnp.bfloat16)
    grad_value = (grad_product * key_gate.astype(jnp.float32)).astype(jnp.bfloat16)
    long_part = filter_partial(long_ext, grad_mixed)
    short_part = filter_partial(short_ext, grad_conv)
    grad_long = lax.psum_scatter(long_part, "seq", scatter_dimension=0, tiled=True)
    grad_short = lax.psum(short_part, "seq")
    return (grad_query, grad_key, grad_value, grad_long, grad_short)


def solution(mesh):
    in_specs = (
        P("seq", "chan"),
        P("seq", "chan"),
        P("seq", "chan"),
        P(("seq", "chan"), None),
        P(None, "chan"),
        P(None, "chan"),
    )
    out_specs = (
        P("seq", "chan"),
        P("seq", "chan"),
        P("seq", "chan"),
        P("seq", "chan"),
        P(None, "chan"),
    )
    return jax.shard_map(body, mesh=mesh, in_specs=in_specs, out_specs=out_specs, check_vma=False)
```

profile of v0, /device:TPU:8, one launch (start us, length us, event | category | flops | bytes accessed | tf_op | source)
XLA Modules:
  0.0 632.7 jit_solution(11481029039536911054)
XLA Ops:
  7.2 1.1 copy.87
  8.4 17.2 %all_to_all.13 = bf16[32,8,1024]{2,0,1:T(8,128)(2,1)S(1)} all-to-all(bf16[32,8,1024]{2,0,1:T(8,128)(2,1)S(1)} %bitcast.63), channel_id=1, replica_groups=mesh['seq'=64,'chan'=8] {'chan'}, dimensions={1} | all-to-all | bytes 1048576 | tf_op jit(solution)/shard_map/all_to_all | solution.py:43
  25.8 1.4 collective-permute-start.2
  27.2 8.3 %collective-permute-done.2 = bf16[127,1024]{1,0:T(8,128)(2,1)S(1)} collective-permute-done((bf16[127,1024]{1,0:T(8,128)(2,1)S(1)}, bf16[127,1024]{1,0:T(8,128)(2,1)S(1)}, u32[]{:S(2)}, u32[]{:S(2)}) %collective-permute-start.2) | collective-permute-done | bytes 260128 | tf_op jit(solution)/shard_map/ppermute | solution.py:10
  35.5 14.2 %fusion.2 = bf16[1,256,1024]{2,0,1:T(2,128)(2,1)S(1)} fusion(bf16[1,383,1024]{2,1,0:T(8,128)(2,1)S(1)} %maximum_bitcast_fusion.1, bf16[128,1,1024]{2,0,1:T(8,128)(2,1)S(1)} %bitcast.65), kind=kOutput, calls=%fused_computation.4 | convolution fusion | flops 67371008 | bytes 1570816 | tf_op jit(solution)/shard_map/conv_general_dilated | solution.py:15
  49.8 1.3 collective-permute-start.3
  51.3 4.2 collective-permute-done.3
  55.7 0.3 copy.48
  56.2 0.6 convolution_select_fusion
  56.8 0.6 copy.50
  57.6 2.6 fusion.14
  60.3 1.8 collective-permute-start
  62.3 2.6 rev.17
  64.9 1.3 dynamic-slice
  67.0 2.5 fusion.12
  70.3 0.6 fusion.5
  71.6 3.8 collective-permute-start.1
  75.4 278.3 %psum.7 = f32[7,1024]{1,0:T(8,128)} all-reduce(f32[7,1024]{1,0:T(8,128)S(1)} %rev.19), channel_id=1, replica_groups=mesh['seq'=64,'chan'=8] {'seq'}, use_global_device_ids=true, to_apply=%region_1.2 | all-reduce | flops 7168 | bytes 57344 | tf_op jit(solution)/shard_map/psum | solution.py:66
  353.9 13.9 %fusion.8 = f32[1,128,1024]{2,0,1:T(1,128)S(1)} fusion(bf16[1,383,1024]{2,1,0:T(8,128)(2,1)S(1)} %maximum_bitcast_fusion, bf16[256,1,1024]{2,0,1:T(8,128)(2,1)S(1)} %bitcast.60), kind=kOutput, calls=%fused_computation.12 | convolution fusion | flops 67108864 | bytes 1832960 | tf_op jit(solution)/shard_map/conv_general_dilated | solution.py:15
  367.9 2.7 rev.18
  370.6 14.2 %fusion.10 = f32[1,256,1024]{2,0,1:T(1,128)S(1)} fusion(bf16[1,383,1024]{2,1,0:T(8,128)(2,1)S(1)} %maximum_bitcast_fusion, bf16[128,1,1024]{2,0,1:T(8,128)(2,1)S(1)} %bitcast.66), kind=kOutput, calls=%fused_computation.14 | convolution fusion | flops 67108864 | bytes 2095104 | tf_op jit(solution)/shard_map/conv_general_dilated | solution.py:15
  384.8 1.1 fusion.17
  385.9 238.6 %all-reduce.3.cloned.1.call-done = f32[128,1024]{1,0:T(8,128)} async-done(((f32[128,1024]{1,0:T(8,128)}), f32[128,1024]{1,0:T(8,128)}) %all-reduce.3.cloned.1.call-update) | async-done | bytes 524304
  624.4 1.4 constant_dynamic-slice_fusion
  (46 shorter events, 3.1 us)
Async XLA Ops:
  7.2 18.4 %copy-start.2 = (bf16[256,1024]{1,0:T(8,128)(2,1)S(1)}, bf16[256,1024]{1,0:T(8,128)(2,1)}, u32[]{:S(2)}) copy-start(bf16[256,1024]{1,0:T(8,128)(2,1)} %param.8) | copy-start | bytes 1572868
  7.2 617.3 %all-reduce.3.cloned.1.call-start = ((), (), s32[]{:S(2)}) async-start(), calls=%async_computation.1 | async-start | bytes 1048576
  25.7 9.8 %copy-start.3 = (bf16[128,1024]{1,0:T(8,128)(2,1)S(1)}, bf16[128,1024]{1,0:T(8,128)(2,1)}, u32[]{:S(2)}) copy-start(bf16[128,1024]{1,0:T(8,128)(2,1)} %param.11) | copy-start | bytes 786436
  25.8 9.7 %collective-permute-start.2 = (bf16[127,1024]{1,0:T(8,128)(2,1)S(1)}, bf16[127,1024]{1,0:T(8,128)(2,1)S(1)}, u32[]{:S(2)}, u32[]{:S(2)}) collective-permute-start(bf16[127,1024]{1,0:T(8,128)(2,1)S(1)} %slice.33), channel_id=1, source_target_pairs={{8,0},{16,8},{24,16},{32,24},{40,32},{48,40},{56,48},{64,56},{72,6... | collective-permute-start | bytes 780296 | tf_op jit(solution)/shard_map/ppermute | solution.py:10
  49.7 5.7 copy-start
  49.8 5.6 collective-permute-start.3
  55.5 0.7 copy-start.6
  55.5 0.7 copy-start.7
  57.6 4.7 copy-start.4
  60.2 6.7 %copy-start.1 = (bf16[1,256,1024]{2,0,1:T(2,128)(2,1)S(1)}, bf16[1,256,1024]{2,0,1:T(2,128)(2,1)}, u32[]{:S(2)}) copy-start(bf16[1,256,1024]{2,0,1:T(2,128)(2,1)} %copy-done) | copy-start | bytes 1572868
  60.3 6.6 %collective-permute-start = (bf16[6,1024]{1,0:T(8,128)(2,1)S(1)}, bf16[6,1024]{1,0:T(8,128)(2,1)S(1)}, u32[]{:S(2)}, u32[]{:S(2)}) collective-permute-start(bf16[6,1024]{1,0:T(8,128)(2,1)S(1)} %slice.29), channel_id=1, source_target_pairs={{0,8},{8,16},{16,24},{24,32},{32,40},{40,48},{48,56},{56,64},{64,7... | collective-permute-start | bytes 36872 | tf_op jit(solution)/shard_map/ppermute | solution.py:10
  71.6 282.2 %collective-permute-start.1 = (bf16[127,1024]{1,0:T(8,128)(2,1)S(1)}, bf16[127,1024]{1,0:T(8,128)(2,1)S(1)}, u32[]{:S(2)}, u32[]{:S(2)}) collective-permute-start(bf16[127,1024]{1,0:T(8,128)(2,1)S(1)} %slice_bitcast_fusion.2), channel_id=1, source_target_pairs={{0,8},{8,16},{16,24},{24,32},{32,40},{40,48},{48,56},{56,64},{64,7... | collective-permute-start | bytes 780296 | tf_op jit(solution)/shard_map/ppermute | solution.py:10
  367.8 2.8 copy-start.5
Sparse Core Ops, SparseCore 0:
  370.7 253.6 all-reduce.2
where the time goes:
time: 633 us
  blocking collectives  296 us (47%)
  waiting for transfers between devices  251 us (40%)
  matrix products  46 us (7%)
  between operations  15.1 us (2%)
  local copies, waits for them, and re-layouts  12.5 us (2%)
  starting transfers between devices  8.33 us (1%)
    psum x1, blocking collectives, body(): grad_short = lax.psum(short_part, 'seq')  278 us
    unnamed x2, waiting for transfers between devices  239 us
    conv_general_dilated x6, matrix products, depthwise(): lax.conv_general_dilated(extended[None], kernel, (1,), [(0, 0)], dimensio...  46 us
    all_to_all x1, blocking collectives, body(): lax.all_to_all(grad_output, 'chan', split_axis=1, concat_axis=0, tiled=True)  17.2 us
  transfers between devices with their start and end apart: 5, of which 3 were waited for; matrix products, arithmetic and copies ran while one was open for 3% of the time, Pallas kernels for 0%

commit v1 on v0

--- a/solution.py
+++ b/solution.py
@@ -2,6 +2,12 @@
 import jax.numpy as jnp
 from jax import lax
 from jax.sharding import PartitionSpec as P
+
+
+def gather_and_add(value, name):
+    parts = lax.all_gather(value, name, axis=0, tiled=False)
+    total = parts.sum(axis=0)
+    return total
 
 
 def passed_along(shard, axis, by):
@@ -63,7 +69,7 @@
     long_part = filter_partial(long_ext, grad_mixed)
     short_part = filter_partial(short_ext, grad_conv)
     grad_long = lax.psum_scatter(long_part, "seq", scatter_dimension=0, tiled=True)
-    grad_short = lax.psum(short_part, "seq")
+    grad_short = gather_and_add(short_part, "seq")
     return (grad_query, grad_key, grad_value, grad_long, grad_short)
 
 

time: 633 us -> 510 us (0.81)
  blocking collectives: 296 us -> 17.2 us
  waiting for transfers between devices: 251 us -> 404 us
    psum x1 -> x0, blocking collectives: 278 us -> none  [body(): grad_short = lax.psum(short_part, 'seq')]
    all_gather x0 -> x1, waiting for transfers between devices: none -> 138 us  [gather_and_add(): parts = lax.all_gather(value, name, axis=0, tiled=False)]
    unnamed x2 -> x3, waiting for transfers between devices: 239 us -> 248 us
  transfers between devices with their start and end apart: 5 -> 6, of which waited for: 3 -> 6; matrix products, arithmetic and copies ran while one was open for 3% -> 5% of each run, Pallas kernels for 0% -> 0%
where the time goes in v1:
time: 510 us
  waiting for transfers between devices  404 us (79%)
  matrix products  46 us (9%)
  blocking collectives  17.2 us (3%)
  between operations  15.1 us (3%)
  local copies, waits for them, and re-layouts  12.4 us (2%)
  starting transfers between devices  8.83 us (2%)
  other arithmetic  6.55 us (1%)
    unnamed x3, waiting for transfers between devices  248 us
    all_gather x1, waiting for transfers between devices, gather_and_add(): parts = lax.all_gather(value, name, axis=0, tiled=False)  138 us
    conv_general_dilated x6, matrix products, depthwise(): lax.conv_general_dilated(extended[None], kernel, (1,), [(0, 0)], dimensio...  46 us
    ppermute x4, waiting for transfers between devices, passed_along(): return lax.ppermute(shard, axis, pairs)  17.4 us
    all_to_all x1, blocking collectives, body(): lax.all_to_all(grad_output, 'chan', split_axis=1, concat_axis=0, tiled=True)  17.2 us
  transfers between devices with their start and end apart: 6, of which 6 were waited for; matrix products, arithmetic and copies ran while one was open for 5% of the time, Pallas kernels for 0%

profile of v1, /device:TPU:8, one launch (start us, length us, event | category | flops | bytes accessed | tf_op | source)
XLA Modules:
  0.0 509.9 jit_solution(9885496614068587305)
XLA Ops:
  7.2 1.1 copy.87
  8.4 17.2 %all_to_all.13 = bf16[32,8,1024]{2,0,1:T(8,128)(2,1)S(1)} all-to-all(bf16[32,8,1024]{2,0,1:T(8,128)(2,1)S(1)} %bitcast.64), channel_id=1, replica_groups=mesh['seq'=64,'chan'=8] {'chan'}, dimensions={1} | all-to-all | bytes 1048576 | tf_op jit(solution)/shard_map/all_to_all | solution.py:49
  25.8 1.4 collective-permute-start.2
  27.2 8.3 %collective-permute-done.2 = bf16[127,1024]{1,0:T(8,128)(2,1)S(1)} collective-permute-done((bf16[127,1024]{1,0:T(8,128)(2,1)S(1)}, bf16[127,1024]{1,0:T(8,128)(2,1)S(1)}, u32[]{:S(2)}, u32[]{:S(2)}) %collective-permute-start.2) | collective-permute-done | bytes 260128 | tf_op jit(solution)/shard_map/ppermute | solution.py:16
  35.5 14.2 %fusion.2 = bf16[1,256,1024]{2,0,1:T(2,128)(2,1)S(1)} fusion(bf16[1,383,1024]{2,1,0:T(8,128)(2,1)S(1)} %maximum_bitcast_fusion.1, bf16[128,1,1024]{2,0,1:T(8,128)(2,1)S(1)} %bitcast.66), kind=kOutput, calls=%fused_computation.4 | convolution fusion | flops 67371008 | bytes 1570816 | tf_op jit(solution)/shard_map/conv_general_dilated | solution.py:21
  49.8 1.3 collective-permute-start.3
  51.3 4.2 collective-permute-done.3
  56.8 0.6 copy.50
  57.6 2.6 fusion.14
  60.2 1.6 collective-permute-start
  62.1 1.2 collective-permute-done
  65.2 4.2 collective-permute-start.1
  69.5 3.8 collective-permute-done.1
  73.4 13.9 %fusion.8 = f32[1,128,1024]{2,0,1:T(1,128)S(1)} fusion(bf16[1,383,1024]{2,1,0:T(8,128)(2,1)S(1)} %maximum_bitcast_fusion, bf16[256,1,1024]{2,0,1:T(8,128)(2,1)S(1)} %bitcast.61), kind=kOutput, calls=%fused_computation.12 | convolution fusion | flops 67108864 | bytes 1832960 | tf_op jit(solution)/shard_map/conv_general_dilated | solution.py:21
  87.4 2.6 rev.18
  90.3 2.5 fusion.12
  92.9 2.4 rev.19
  95.7 1.3 dynamic-slice
  97.6 14.2 %fusion.10 = f32[1,256,1024]{2,0,1:T(1,128)S(1)} fusion(bf16[1,383,1024]{2,1,0:T(8,128)(2,1)S(1)} %maximum_bitcast_fusion, bf16[128,1,1024]{2,0,1:T(8,128)(2,1)S(1)} %bitcast.67), kind=kOutput, calls=%fused_computation.14 | convolution fusion | flops 67108864 | bytes 2095104 | tf_op jit(solution)/shard_map/conv_general_dilated | solution.py:21
  111.8 1.1 fusion.17
  112.9 248.4 %all-reduce.3.cloned.1.call-done = f32[128,1024]{1,0:T(8,128)} async-done(((f32[128,1024]{1,0:T(8,128)}), f32[128,1024]{1,0:T(8,128)}) %all-reduce.3.cloned.1.call-update) | async-done | bytes 524304
  361.3 1.4 constant_dynamic-slice_fusion
  362.6 138.0 %all-gather.4.cloned.1.call-done = f32[64,7,1024]{2,1,0:T(8,128)} async-done(((f32[1,7,1024]{2,1,0:T(8,128)}), f32[64,7,1024]{2,1,0:T(8,128)}) %all-gather.4.cloned.1.call-update) | async-done | bytes 1835024 | tf_op jit(solution)/shard_map/all_gather | solution.py:8
  500.6 2.4 reduce_sum.9
  (47 shorter events, 5.0 us)
Async XLA Ops:
  7.2 18.4 %copy-start.2 = (bf16[256,1024]{1,0:T(8,128)(2,1)S(1)}, bf16[256,1024]{1,0:T(8,128)(2,1)}, u32[]{:S(2)}) copy-start(bf16[256,1024]{1,0:T(8,128)(2,1)} %param.8) | copy-start | bytes 1572868
  7.2 354.1 %all-reduce.3.cloned.1.call-start = ((), (), s32[]{:S(2)}) async-start(), calls=%async_computation.2 | async-start | bytes 1048576
  25.7 9.8 %copy-start.3 = (bf16[128,1024]{1,0:T(8,128)(2,1)S(1)}, bf16[128,1024]{1,0:T(8,128)(2,1)}, u32[]{:S(2)}) copy-start(bf16[128,1024]{1,0:T(8,128)(2,1)} %param.11) | copy-start | bytes 786436
  25.8 9.7 %collective-permute-start.2 = (bf16[127,1024]{1,0:T(8,128)(2,1)S(1)}, bf16[127,1024]{1,0:T(8,128)(2,1)S(1)}, u32[]{:S(2)}, u32[]{:S(2)}) collective-permute-start(bf16[127,1024]{1,0:T(8,128)(2,1)S(1)} %slice.33), channel_id=1, source_target_pairs={{8,0},{16,8},{24,16},{32,24},{40,32},{48,40},{56,48},{64,56},{72,6... | collective-permute-start | bytes 780296 | tf_op jit(solution)/shard_map/ppermute | solution.py:16
  49.7 5.7 %copy-start = (bf16[1,256,1024]{2,0,1:T(2,128)(2,1)}, bf16[1,256,1024]{2,0,1:T(2,128)(2,1)S(1)}, u32[]{:S(2)}) copy-start(bf16[1,256,1024]{2,0,1:T(2,128)(2,1)S(1)} %fusion.2) | copy-start | bytes 1572868
  49.8 5.6 %collective-permute-start.3 = (bf16[6,1024]{1,0:T(8,128)(2,1)S(1)}, bf16[6,1024]{1,0:T(8,128)(2,1)S(1)}, u32[]{:S(2)}, u32[]{:S(2)}) collective-permute-start(bf16[6,1024]{1,0:T(8,128)(2,1)S(1)} %bitcast.72), channel_id=1, source_target_pairs={{8,0},{16,8},{24,16},{32,24},{40,32},{48,40},{56,48},{64,56},{72,6... | collective-permute-start | bytes 36872 | tf_op jit(solution)/shard_map/ppermute | solution.py:16
  55.5 0.7 copy-start.5
  55.5 0.7 copy-start.6
  60.2 3.1 collective-permute-start
  65.2 8.1 %collective-permute-start.1 = (bf16[127,1024]{1,0:T(8,128)(2,1)S(1)}, bf16[127,1024]{1,0:T(8,128)(2,1)S(1)}, u32[]{:S(2)}, u32[]{:S(2)}) collective-permute-start(bf16[127,1024]{1,0:T(8,128)(2,1)S(1)} %slice_bitcast_fusion.2), channel_id=1, source_target_pairs={{0,8},{8,16},{16,24},{24,32},{32,40},{40,48},{48,56},{56,64},{64,7... | collective-permute-start | bytes 780296 | tf_op jit(solution)/shard_map/ppermute | solution.py:16
  87.3 3.0 copy-start.1
  90.1 5.3 %copy-start.4 = (bf16[128,1024]{1,0:T(8,128)(2,1)S(1)}, bf16[128,1024]{1,0:T(8,128)(2,1)}, u32[]{:S(2)}) copy-start(bf16[128,1024]{1,0:T(8,128)(2,1)} %param.11) | copy-start | bytes 786436
  90.1 410.5 %all-gather.4.cloned.1.call-start = ((), (), s32[]{:S(2)}) async-start(), calls=%async_computation.1 | async-start | bytes 2129920 | tf_op jit(solution)/shard_map/all_gather | solution.py:8
Sparse Core Ops, SparseCore 0:
  90.2 271.0 all-reduce.2
  365.2 135.3 all-gather.3
